TPU v7x, 1024 devices: a whole 8x8x8 slice. The times are simulated.
1024 devices in a mesh: wide: 32 (over z, y_lo), narrow: 32 (over y_hi, x, core).
Axes of the slice: x: 8, y: 8 (y_hi: 2, y_lo: 4; y = y_hi * 4 + y_lo), z: 8, core: 2. Of those that a mesh axis runs over, the one named last changes fastest.
Arguments:
- tokens: bfloat16 [131072, 4096], P(('wide', 'narrow')), may hold values from -24 to 24
- norm_gain: bfloat16 [4096], P('narrow'), may hold values from 0.099609375 to 1.8984375
- key_weight: bfloat16 [4096, 512], P('narrow'), may hold values from -0.09375 to 0.09375
- key_grad: bfloat16 [131072, 512], P(('wide', 'narrow')), may hold values from -6 to 6
Outputs:
- keys: bfloat16 [131072, 512], P(('wide', 'narrow'))
- weight_grad: float32 [4096, 512], P('narrow')
- gain_grad: float32 [4096], P('narrow')
All inputs are finite; a program needn't handle non-finite values.
Results may differ from a plain program's by a relative error of at most 0.0057.
Values may be sent and summed in bfloat16 or wider, within the bound.
A program may use at most 32 MiB of HBM per device.

v0:
```python
import math

import jax
import jax.numpy as jnp
from jax import lax
from jax.sharding import PartitionSpec as P

KH = 4
HD = 128
KV = 512
SEQ = 4096


rope_base = 500000.0
norm_eps = 1e-05


def rope_tables(first_row, row_count, head_size):
    position = ((first_row + jnp.arange(row_count, dtype=jnp.int32)) % SEQ).astype(jnp.float32)
    halves = jnp.arange(head_size // 2, dtype=jnp.float32)
    frequency = rope_base ** (-2.0 * halves / head_size)
    angle = position[:, None] * frequency[None, :]
    return (jnp.cos(angle), jnp.sin(angle))


def rotate_keys(projected, cosine, sine_table):
    rows = projected.shape[0]
    heads = projected.reshape(rows, KH, HD)
    front_half = heads[:, :, : HD // 2]
    back_half = heads[:, :, HD // 2 :]
    cosine = cosine[:, None, :]
    sine_table = sine_table[:, None, :]
    joined = jnp.concatenate(
        [
            front_half * cosine - back_half * sine_table,
            back_half * cosine + front_half * sine_table,
        ],
        axis=2,
    )
    return joined.reshape(rows, KV)


def rotate_back(upstream, cosine, sine_table):
    rows = upstream.shape[0]
    heads = upstream.reshape(rows, KH, HD)
    grad_front = heads[:, :, : HD // 2]
    grad_back = heads[:, :, HD // 2 :]
    cosine = cosine[:, None, :]
    sine_table = sine_table[:, None, :]
    joined = jnp.concatenate(
        [
            grad_front * cosine + grad_back * sine_table,
            grad_back * cosine - grad_front * sine_table,
        ],
        axis=2,
    )
    return joined.reshape(rows, KV)


def local(tokens, norm_gain, key_weight, key_grad):
    row_count = tokens.shape[0]
    narrow_size = lax.axis_size("narrow")
    wide_size = lax.axis_size("wide")
    first_row = (lax.axis_index("wide") * narrow_size + lax.axis_index("narrow")) * row_count
    grad_scale = 1.0 / math.sqrt(row_count * narrow_size * wide_size)
    widened = tokens.astype(jnp.float32)
    inv_rms = lax.rsqrt(jnp.mean(widened * widened, axis=1, keepdims=True) + norm_eps)
    normed = widened * inv_rms
    cosine, sine_table = rope_tables(first_row, row_count, HD)
    pre_grad = rotate_back(key_grad.astype(jnp.float32), cosine, sine_table).astype(jnp.bfloat16)
    gain_wide, weight_wide = (
        lax.all_gather(norm_gain, "narrow", axis=0, tiled=True),
        lax.all_gather(key_weight, "narrow", axis=0, tiled=True),
    )
    hidden_in = (normed * gain_wide.astype(jnp.float32)[None, :]).astype(jnp.bfloat16)
    projected = jnp.dot(hidden_in, weight_wide, preferred_element_type=jnp.float32)
    hidden_grad = lax.dot_general(
        pre_grad, weight_wide, (((1,), (1,)), ((), ())), preferred_element_type=jnp.float32
    )
    keys = rotate_keys(projected, cosine, sine_table).astype(jnp.bfloat16)
    weight_term = (
        lax.dot_general(
            hidden_in, pre_grad, (((0,), (0,)), ((), ())), preferred_element_type=jnp.float32
        )
        * grad_scale
    )
    weight_part = weight_term.astype(jnp.bfloat16)
    gain_term = jnp.sum(hidden_grad * normed, axis=0) * grad_scale
    model_width = weight_part.shape[0]
    own_rows = model_width // narrow_size
    half_cols = KV // 2
    front_part = weight_part[:, :half_cols].reshape(narrow_size, own_rows, half_cols)
    back_part = weight_part[:, half_cols:].reshape(narrow_size, own_rows, half_cols)
    front_recv = lax.all_to_all(front_part, "narrow", split_axis=0, concat_axis=0, tiled=True)
    back_recv = lax.all_to_all(back_part, "narrow", split_axis=0, concat_axis=0, tiled=True)
    front_sum = jnp.sum(front_recv.astype(jnp.float32), axis=0)
    back_sum = jnp.sum(back_recv.astype(jnp.float32), axis=0)
    weight_rows = jnp.concatenate([front_sum, back_sum], axis=1)
    gain_rows = lax.psum_scatter(gain_term, "narrow", scatter_dimension=0, tiled=True)
    weight_grad, gain_grad = lax.psum((weight_rows, gain_rows), "wide")
    return (keys, weight_grad, gain_grad)


def solution(mesh):
    return jax.shard_map(
        local,
        mesh=mesh,
        in_specs=(
            P(("wide", "narrow"), None),
            P("narrow"),
            P("narrow", None),
            P(("wide", "narrow"), None),
        ),
        out_specs=(P(("wide", "narrow"), None), P("narrow", None), P("narrow")),
        check_vma=False,
    )
```

profile of v0, /device:TPU:10, one launch (start us, length us, event | category | flops | bytes accessed | tf_op | source)
XLA Modules:
  0.0 584.2 jit_solution(11283645883743272540)
XLA Ops:
  7.2 0.0 all-gather.3.cloned.1.call-start
  7.2 0.7 all-gather.3.cloned.1.call-update
  7.9 46.1 %all-gather = bf16[32,1,128]{2,1,0:T(2,128)(2,1)S(1)} all-gather(bf16[1,1,128]{2,1,0:T(2,128)(2,1)} %bitcast.25), channel_id=1, replica_groups=mesh['wide'=32,'narrow'=32] {'narrow'}, dimensions={0}, use_global_device_ids=true | all-gather | bytes 8448 | tf_op jit(solution)/shard_map/all_gather | solution.py:72
  54.0 1.0 reshape.108
  55.0 1.5 fusion.2
  56.6 0.3 multiply_cosine_fusion
  56.9 74.9 %all-gather.3.cloned.1.call-done = bf16[4096,512]{1,0:T(8,128)(2,1)} async-done(((bf16[128,512]{1,0:T(8,128)(2,1)}), bf16[4096,512]{1,0:T(8,128)(2,1)}) %all-gather.3.cloned.1.call-update) | async-done | bytes 4194320 | tf_op jit(solution)/shard_map/all_gather | solution.py:73
  131.8 3.3 fusion.5
  135.1 0.0 copy-start
  135.1 0.1 reshape.102
  135.2 0.4 add_convert_fusion
  135.6 0.4 pad_maximum_fusion.1
  136.0 0.3 copy-done
  136.3 1.4 multiply_convert_fusion
  137.7 1.6 fusion.13
  139.3 59.0 %all_to_all.10 = bf16[32,128,256]{2,1,0:T(8,128)(2,1)} all-to-all(bf16[32,128,256]{2,1,0:T(8,128)(2,1)S(1)} %bitcast.18), channel_id=1, replica_groups=mesh['wide'=32,'narrow'=32] {'narrow'}, dimensions={0} | all-to-all | bytes 4194304 | tf_op jit(solution)/shard_map/all_to_all | solution.py:95
  198.3 6.8 %all-to-all-start = ((bf16[32,128,256]{2,1,0:T(8,128)(2,1)}), bf16[32,128,256]{2,1,0:T(8,128)(2,1)S(1)}, u32[]{:S(2)}, u32[]{:S(2)}) async-start(bf16[32,128,256]{2,1,0:T(8,128)(2,1)} %bitcast.17), calls=%async_computation | async-start | bytes 4194304 | tf_op jit(solution)/shard_map/all_to_all | solution.py:94
  205.1 0.0 all-reduce.3.cloned.1.call-start
  205.2 1.3 dynamic-slice
  207.1 1.9 convert_reduce_fusion
  209.0 47.0 %all-to-all-done = bf16[32,128,256]{2,1,0:T(8,128)(2,1)S(1)} async-done(((bf16[32,128,256]{2,1,0:T(8,128)(2,1)}), bf16[32,128,256]{2,1,0:T(8,128)(2,1)S(1)}, u32[]{:S(2)}, u32[]{:S(2)}) %all-to-all-start) | async-done | bytes 2097184 | tf_op jit(solution)/shard_map/all_to_all | solution.py:94
  256.0 0.3 convert_reduce_fusion.1
  256.3 0.7 pad_maximum_fusion
  257.0 0.0 all-reduce.3.cloned.1.call-update
  257.1 3.7 fusion.3
  260.8 0.7 copy.18
  261.4 145.6 %all-reduce = f32[4096]{0:T(1024)S(1)} all-reduce(f32[4096]{0:T(1024)S(1)} %broadcast_multiply_fusion), channel_id=2, replica_groups=mesh['wide'=32,'narrow'=32] {'narrow'}, use_global_device_ids=true, to_apply=%region_5.6.clone | all-reduce | flops 4096 | bytes 32768
  407.1 0.1 dynamic-slice.1
  407.1 81.3 %psum.15 = f32[128]{0:T(128)} all-reduce(f32[128]{0:T(128)S(1)} %dynamic-slice.1), channel_id=1, replica_groups=mesh['wide'=32,'narrow'=32] {'wide'}, use_global_device_ids=true, to_apply=%region_6.7 | all-reduce | flops 128 | bytes 1024 | tf_op jit(solution)/shard_map/psum | solution.py:100
  488.4 87.3 %all-reduce.3.cloned.1.call-done = f32[128,512]{1,0:T(8,128)} async-done(((f32[128,512]{1,0:T(8,128)}), f32[128,512]{1,0:T(8,128)}) %all-reduce.3.cloned.1.call-update) | async-done | bytes 262160 | tf_op jit(solution)/shard_map/psum | solution.py:100
  575.7 1.7 copy.20
  (5 shorter events, 0.1 us)
Async XLA Ops:
  7.2 124.6 %all-gather.3.cloned.1.call-start = ((), (), s32[]{:S(2)}) async-start(), calls=%async_computation.2 | async-start | bytes 4325376 | tf_op jit(solution)/shard_map/all_gather | solution.py:73
  135.1 1.2 copy-start
  198.3 57.8 %all-to-all-start = ((bf16[32,128,256]{2,1,0:T(8,128)(2,1)}), bf16[32,128,256]{2,1,0:T(8,128)(2,1)S(1)}, u32[]{:S(2)}, u32[]{:S(2)}) async-start(bf16[32,128,256]{2,1,0:T(8,128)(2,1)} %bitcast.17), calls=%async_computation | async-start | bytes 4194304 | tf_op jit(solution)/shard_map/all_to_all | solution.py:94
  205.1 370.6 %all-reduce.3.cloned.1.call-start = ((), (), s32[]{:S(2)}) async-start(), calls=%async_computation.3 | async-start | bytes 524288 | tf_op jit(solution)/shard_map/psum | solution.py:100
Sparse Core Ops, SparseCore 0:
  12.5 119.2 all-gather.2
  257.2 318.4 all-reduce.2
where the time goes:
time: 585 us; the launch traced here: 584 us
  blocking collectives  332 us (57%)
  waiting for transfers between devices  210 us (36%)
  between operations  14.8 us (3%)
  matrix products  8.35 us (1%)
  starting transfers between devices  6.93 us (1%)
  local copies, waits for them, and re-layouts  6.69 us (1%)
    unnamed x1, blocking collectives  146 us
    psum x1, waiting for transfers between devices, local(): weight_grad, gain_grad = lax.psum((weight_rows, gain_rows), 'wide')  87.3 us
    psum x1, blocking collectives, local(): weight_grad, gain_grad = lax.psum((weight_rows, gain_rows), 'wide')  81.3 us
    all_gather x1, waiting for transfers between devices, local(): lax.all_gather(key_weight, 'narrow', axis=0, tiled=True)  74.9 us
    all_to_all x1, blocking collectives, local(): lax.all_to_all(back_part, 'narrow', split_axis=0, concat_axis=0, tiled=True)  59 us
    all_to_all x1, waiting for transfers between devices, local(): lax.all_to_all(front_part, 'narrow', split_axis=0, concat_axis=0, tiled=T...  47 us
    all_gather x1, blocking collectives, local(): lax.all_gather(norm_gain, 'narrow', axis=0, tiled=True)  46.1 us
  transfers between devices with their start and end apart: 3, of which 3 were waited for; matrix products, arithmetic and copies ran while one was open for 2% of the time, Pallas kernels for 0%

commit v1 on v0

v1 whole, which is shorter than its diff:
```python
import math

import jax
import jax.numpy as jnp
from jax import lax
from jax.sharding import PartitionSpec as P

KH = 4
HD = 128
KV = 512
SEQ = 4096

rope_base = 500000.0
norm_eps = 1e-05


def rope_tables(first_row, row_count, head_size):
    position = ((first_row + jnp.arange(row_count, dtype=jnp.int32)) % SEQ).astype(jnp.float32)
    halves = jnp.arange(head_size // 2, dtype=jnp.float32)
    frequency = rope_base ** (-2.0 * halves / head_size)
    angle = position[:, None] * frequency[None, :]
    return (jnp.cos(angle), jnp.sin(angle))


def rotate(values, cosine, sine_table):
    rows = values.shape[0]
    heads = values.reshape(rows, KH, HD)
    front_half = heads[:, :, : HD // 2]
    back_half = heads[:, :, HD // 2 :]
    cosine = cosine[:, None, :]
    sine_table = sine_table[:, None, :]
    joined = jnp.concatenate(
        [
            front_half * cosine - back_half * sine_table,
            back_half * cosine + front_half * sine_table,
        ],
        axis=2,
    )
    return joined.reshape(rows, KV)


def local(tokens, norm_gain, key_weight, key_grad):
    row_count = tokens.shape[0]
    narrow_size = lax.axis_size("narrow")
    wide_size = lax.axis_size("wide")
    first_row = (lax.axis_index("wide") * narrow_size + lax.axis_index("narrow")) * row_count
    grad_scale = 1.0 / math.sqrt(row_count * narrow_size * wide_size)
    gain_col = norm_gain.astype(jnp.float32)[:, None]
    gained = (gain_col * key_weight.astype(jnp.float32)).astype(jnp.bfloat16)
    gained_wide = lax.all_gather(gained, "narrow", axis=0, tiled=True)
    widened = tokens.astype(jnp.float32)
    inv_rms = lax.rsqrt(jnp.mean(widened * widened, axis=1, keepdims=True) + norm_eps)
    cosine, sine_table = rope_tables(first_row, row_count, HD)
    pre_grad = rotate(key_grad.astype(jnp.float32), cosine, -sine_table)
    scaled_grad = (pre_grad * inv_rms).astype(jnp.bfloat16)
    part = lax.dot_general(
        tokens, scaled_grad, (((0,), (0,)), ((), ())), preferred_element_type=jnp.float32
    ).astype(jnp.bfloat16)
    part = part.reshape(narrow_size, part.shape[0] // narrow_size, KV)
    recv = lax.all_to_all(part, "narrow", split_axis=0, concat_axis=0, tiled=True)
    rows = jnp.sum(recv.astype(jnp.float32), axis=0) * grad_scale
    total = lax.psum(rows, "wide")
    projected = jnp.dot(tokens, gained_wide, preferred_element_type=jnp.float32) * inv_rms
    keys = rotate(projected, cosine, sine_table).astype(jnp.bfloat16)
    weight_grad = total * gain_col
    gain_grad = jnp.sum(total * key_weight.astype(jnp.float32), axis=1)
    return (keys, weight_grad, gain_grad)


def solution(mesh):
    return jax.shard_map(
        local,
        mesh=mesh,
        in_specs=(
            P(("wide", "narrow"), None),
            P("narrow"),
            P("narrow", None),
            P(("wide", "narrow"), None),
        ),
        out_specs=(P(("wide", "narrow"), None), P("narrow", None), P("narrow")),
        check_vma=False,
    )
```

time: 585 us -> 579 us (0.990)
  the two profiles are of different devices: /device:TPU:10 before, /device:TPU:1 now
where the time goes in v1:
time: 579 us; the launch traced here: 578 us
  waiting for transfers between devices  435 us (75%)
  blocking collectives  115 us (20%)
  between operations  14.2 us (2%)
  matrix products  5.91 us (1%)
    psum x1, waiting for transfers between devices, local(): total = lax.psum(rows, 'wide')  299 us
    all_gather x1, waiting for transfers between devices, local(): gained_wide = lax.all_gather(gained, 'narrow', axis=0, tiled=True)  136 us
    all_to_all x1, blocking collectives, local(): lax.all_to_all(part, 'narrow', split_axis=0, concat_axis=0, tiled=True)  115 us
  transfers between devices with their start and end apart: 2, of which 2 were waited for; matrix products, arithmetic and copies ran while one was open for 0% of the time, Pallas kernels for 0%

profile of v1, /device:TPU:1, one launch (start us, length us, event | category | flops | bytes accessed | tf_op | source)
XLA Modules:
  0.0 578.5 jit_solution(17644196264680265206)
XLA Ops:
  7.2 0.0 all-reduce.2.cloned.1.call-start
  7.2 1.0 copy.18
  8.3 1.5 multiply_reduce_fusion
  9.8 0.2 fusion.4
  10.1 2.5 fusion
  12.6 1.2 copy.22
  13.7 114.5 %all_to_all.5 = bf16[32,128,512]{1,2,0:T(8,128)(2,1)S(1)} all-to-all(bf16[32,128,512]{1,2,0:T(8,128)(2,1)S(1)} %bitcast.19), channel_id=1, replica_groups=mesh['wide'=32,'narrow'=32] {'narrow'}, dimensions={0} | all-to-all | bytes 8388608 | tf_op jit(solution)/shard_map/all_to_all | solution.py:60
  128.3 0.0 copy-start.1
  128.3 0.0 copy-start.2
  128.3 0.0 copy-start
  128.3 0.6 convert_reduce_fusion
  128.9 0.7 broadcast_multiply_fusion
  129.6 0.0 all-reduce.2.cloned.1.call-update
  129.6 0.0 all-gather.2.cloned.1.call-start
  129.7 0.0 copy-done.1
  129.7 0.1 copy.10
  129.8 0.0 copy-done.2
  129.8 298.9 %all-reduce.2.cloned.1.call-done = f32[128,512]{0,1:T(8,128)} async-done(((f32[128,512]{0,1:T(8,128)}), f32[128,512]{0,1:T(8,128)}) %all-reduce.2.cloned.1.call-update) | async-done | bytes 262160 | tf_op jit(solution)/shard_map/psum | solution.py:62
  428.7 2.2 fusion.2
  430.8 0.0 all-gather.2.cloned.1.call-update
  430.9 0.8 copy.16
  431.7 135.7 %all-gather.2.cloned.1.call-done = bf16[4096,512]{0,1:T(8,128)(2,1)} async-done(((bf16[128,512]{0,1:T(8,128)(2,1)}), bf16[4096,512]{0,1:T(8,128)(2,1)}) %all-gather.2.cloned.1.call-update) | async-done | bytes 4194320 | tf_op jit(solution)/shard_map/all_gather | solution.py:50
  567.4 0.0 copy-done
  567.4 3.4 convolution_multiply_fusion
  570.9 0.8 copy.17
  (9 shorter events, 0.2 us)
Async XLA Ops:
  7.2 421.5 %all-reduce.2.cloned.1.call-start = ((), (), s32[]{:S(2)}) async-start(), calls=%async_computation.2 | async-start | bytes 524288 | tf_op jit(solution)/shard_map/psum | solution.py:62
  128.3 1.4 copy-start.1
  128.3 1.5 copy-start.2
  128.3 439.1 %copy-start = (bf16[128,4096]{1,0:T(8,128)(2,1)S(1)}, bf16[128,4096]{1,0:T(8,128)(2,1)}, u32[]{:S(2)}) copy-start(bf16[128,4096]{1,0:T(8,128)(2,1)} %param.4) | copy-start | bytes 3145732
  129.6 437.7 %all-gather.2.cloned.1.call-start = ((), (), s32[]{:S(2)}) async-start(), calls=%async_computation.1 | async-start | bytes 4325376 | tf_op jit(solution)/shard_map/all_gather | solution.py:50
Sparse Core Ops, SparseCore 0:
  129.7 298.8 all-reduce.1
  434.3 133.0 all-gather.1

commit v2 on v1

v2 whole, which is shorter than its diff:
```python
import functools
import math

import jax
import jax.numpy as jnp
from jax import lax
from jax.experimental import pallas as pl
from jax.experimental.pallas import tpu as pltpu
from jax.sharding import PartitionSpec as P

KH = 4
HD = 128
KV = 512
SEQ = 4096
Y_LO = 4
ROWS = 128

rope_base = 500000.0
norm_eps = 1e-05
MESH = pl.DeviceIdType.MESH
F32 = jnp.float32
BF16 = jnp.bfloat16


def chain_lengths(size):
    return (size // 2, size - 1 - size // 2)


def kernel(
    nx, nz, scale,
    tokens_hbm, gained_ref, key_grad_ref, cos_ref, sin_ref, weight_ref, gain_ref,
    keys_ref, weight_grad_ref, gain_grad_ref,
    tok, mixed, grads, gathered, part_y, part_z, chain_y, chain_z,
    out_x, in_x, in_z, out_y, in_y, final_y, final_z,
    local_sem, own_sem, pair_send, pair_recv, cross_send, cross_recv, far_send, far_recv,
    ring_send, ring_recv, chain_send, chain_recv,
    x_send, x_recv, z_send, z_recv, y_send, y_recv, fy_send, fy_recv, fz_send, fz_recv,
):
    ny = 2 * Y_LO
    wide = lax.axis_index("wide")
    narrow = lax.axis_index("narrow")
    core = lax.rem(narrow, 2)
    px = lax.rem(narrow // 2, nx)
    y_hi = narrow // (2 * nx)
    y_lo = lax.rem(wide, Y_LO)
    pz = wide // Y_LO
    py = y_hi * Y_LO + y_lo
    ry = ROWS // Y_LO
    rz = ROWS // nz
    blocks = 2 * nx

    def device(x, y, z, c):
        return (z * Y_LO + lax.rem(y, Y_LO), ((y // Y_LO) * nx + x) * 2 + c)

    def at_x(k):
        return device(lax.rem(px + k + nx, nx), py, pz, core)

    def at_y(k):
        return device(px, lax.rem(py + k + ny, ny), pz, core)

    def at_z(k):
        return device(px, py, lax.rem(pz + k + nz, nz), core)

    sibling = device(px, py, pz, 1 - core)
    started = []

    def remote(src, dst, send_sem, recv_sem, target):
        return pltpu.make_async_remote_copy(
            src_ref=src, dst_ref=dst, send_sem=send_sem, recv_sem=recv_sem,
            device_id=target, device_id_type=MESH,
        )

    def send(src, dst, send_sem, recv_sem, target):
        copy = remote(src, dst, send_sem, recv_sem, target)
        copy.start()
        started.append(copy)
        return copy

    def slot(hi, x, c):
        return pl.ds(pl.multiple_of(((hi * nx + x) * 2 + c) * ROWS, ROWS), ROWS)

    load = pltpu.make_async_copy(tokens_hbm, tok, local_sem)
    load.start()
    own_rows = pl.ds(pl.multiple_of(core * ROWS, ROWS), ROWS)
    own_loads = []
    for j in range(blocks):
        cols = pl.ds(pl.multiple_of((2 * j + core) * ROWS, ROWS), ROWS)
        copy = pltpu.make_async_copy(tokens_hbm.at[:, cols], mixed.at[j, own_rows, :], own_sem.at[j])
        copy.start()
        own_loads.append(copy)

    barrier = pltpu.get_barrier_semaphore()
    partners = [at_x(k) for k in range(1, nx)] + [at_y(k) for k in range(1, ny)]
    partners += [at_z(k) for k in range(1, nz)] + [sibling]
    for partner in partners:
        pl.semaphore_signal(barrier, inc=1, device_id=partner, device_id_type=MESH)

    gathered[slot(y_hi, px, core), :] = gained_ref[...]
    load.wait()
    squares = jnp.zeros((ROWS, 128), F32)
    for j in range(2 * blocks):
        piece = tok[:, j * 128 : (j + 1) * 128].astype(F32)
        squares = squares + piece * piece
    mean = jnp.sum(squares, axis=1, keepdims=True) * (1.0 / tok.shape[1])
    inv_rms = lax.rsqrt(mean + norm_eps)
    cosine, sine = cos_ref[...], sin_ref[...]
    for h in range(KH):
        head = key_grad_ref[:, h * HD : (h + 1) * HD].astype(F32)
        turned = head * cosine - pltpu.roll(head, HD // 2, 1) * sine
        grads[own_rows, h * HD : (h + 1) * HD] = (turned * inv_rms).astype(BF16)

    pl.semaphore_wait(barrier, len(partners))

    pair = [send(grads.at[own_rows, :], grads.at[own_rows, :], pair_send.at[blocks], pair_recv.at[blocks], sibling)]
    for j in range(blocks):
        cols = pl.ds(pl.multiple_of((2 * j + 1 - core) * ROWS, ROWS), ROWS)
        pair.append(send(tokens_hbm.at[:, cols], mixed.at[j, own_rows, :], pair_send.at[j], pair_recv.at[j], sibling))

    far_slot = slot(1 - y_hi, px, core)
    own_slot = slot(y_hi, px, core)

    def far_copies(sign):
        return [
            remote(gained_ref, gathered.at[own_slot, :], far_send.at[i], far_recv, at_y(sign * (i + 1)))
            for i in range(Y_LO // 2)
        ]

    @pl.when(y_lo == 0)
    def _():
        for copy in far_copies(-1):
            copy.start()

    @pl.when(y_lo == Y_LO - 1)
    def _():
        for copy in far_copies(1):
            copy.start()

    long_x, short_x = chain_lengths(nx)
    ring_steps = [[long_x, short_x], [short_x, long_x]]
    highs = (y_hi, 1 - y_hi)
    ring = {}
    cross = {}

    def ring_step(stream, way, t):
        sign = 1 - 2 * way
        if t > 0:
            ring[stream, way, t - 1].wait_recv()
            share(stream, lax.rem(px - sign * t + nx, nx), (-sign * t) % nx)
        if t < ring_steps[stream][way]:
            rows = slot(highs[stream], lax.rem(px - sign * t + nx, nx), core)
            src = gained_ref if (t == 0 and stream == 0) else gathered.at[rows, :]
            index = (stream, way, t)
            ring[index] = send(src, gathered.at[rows, :], ring_send.at[index], ring_recv.at[index], at_x(sign))

    def share(stream, x, offset):
        rows = slot(highs[stream], x, core)
        src = gained_ref if (offset == 0 and stream == 0) else gathered.at[rows, :]
        cross[stream, offset] = send(
            src, gathered.at[rows, :], cross_send.at[stream, offset], cross_recv.at[stream, offset], sibling
        )

    ring_step(0, 0, 0)
    ring_step(0, 1, 0)
    share(0, px, 0)

    for copy in own_loads:
        copy.wait()
    for copy in pair:
        copy.wait_recv()

    def block_step(j, carry):
        value = lax.dot_general(
            mixed[j], grads[...], (((0,), (0,)), ((), ())), preferred_element_type=F32
        ).astype(BF16)
        hi, x = j // nx, lax.rem(j, nx)
        for s in range(2):
            for i in range(Y_LO):
                part_y[s, hi * Y_LO + i, x] = value[i * ry : (i + 1) * ry, s * 128 : (s + 1) * 128]
            for i in range(nz):
                part_z[s, i, j] = value[i * rz : (i + 1) * rz, 256 + s * 128 : 256 + (s + 1) * 128]
        return carry

    lax.fori_loop(0, blocks, block_step, 0)

    axes = ((ny, py, at_y, part_y, chain_y), (nz, pz, at_z, part_z, chain_z))
    chains = {}

    def chain_steps(size, way, s):
        return chain_lengths(size)[(way + s) % 2]

    def chain_step(axis, way, s, t):
        size, place, at, part, chain = axes[axis]
        steps = chain_steps(size, way, s)
        if t >= steps:
            return
        sign = 1 - 2 * way
        goal = lax.rem(place + sign * (steps - t) + size, size)
        if t > 0:
            chains[axis, way, s, t - 1].wait_recv()
            total = part[s, goal].astype(F32) + chain[way, s, t - 1].astype(F32)
            part[s, goal] = total.astype(BF16)
        index = (axis, way, s, t)
        chains[index] = send(
            part.at[s, goal], chain.at[way, s, t], chain_send.at[index], chain_recv.at[index], at(sign)
        )

    remote(gained_ref, gathered.at[far_slot, :], far_send.at[0], far_recv, sibling).wait_recv()
    longest = max(ny, nz) // 2
    for t in range(longest):
        for s in range(2):
            for axis in range(2):
                for way in range(2):
                    chain_step(axis, way, s, t)
        if t == 0:
            share(1, px, 0)
            ring_step(1, 0, 0)
            ring_step(1, 1, 0)
        else:
            for stream in range(2):
                for way in range(2):
                    if t <= ring_steps[stream][way]:
                        ring_step(stream, way, t)

    for axis in range(2):
        size, place, _, part, chain = axes[axis]
        for s in range(2):
            total = part[s, place].astype(F32)
            for way in range(2):
                steps = chain_steps(size, way, s)
                if steps > 0:
                    chains[axis, way, s, steps - 1].wait_recv()
                    total = total + chain[way, s, steps - 1].astype(F32)
            total = total.astype(BF16)
            if axis == 0:
                out_x[:, s, :ry, :] = total
            else:
                for hi in range(2):
                    out_x[:, s, ry + hi * rz : ry + (hi + 1) * rz, :] = total[hi * nx : (hi + 1) * nx]

    to_x = []
    for k in range(1, nx):
        goal = lax.rem(px + k, nx)
        to_x.append(send(out_x.at[goal], in_x.at[k], x_send.at[k], x_recv.at[k], at_x(k)))

    for t in range(longest, long_x + 1):
        for stream in range(2):
            for way in range(2):
                if t <= ring_steps[stream][way]:
                    ring_step(stream, way, t)

    total = out_x[px].astype(F32)
    for k in range(1, nx):
        to_x[k - 1].wait_recv()
        total = total + in_x[k].astype(F32)
    total = total.astype(BF16)
    in_z[pz] = total[:, :ry, :]
    for hi in range(2):
        out_y[hi] = total[:, ry + hi * rz : ry + (hi + 1) * rz, :]
    in_y[py] = out_y[y_hi]

    to_z = []
    for k in range(1, nz):
        to_z.append(send(in_z.at[pz], in_z.at[pz], z_send.at[k], z_recv.at[k], at_z(k)))
    to_y = []
    for k in range(1, ny):
        goal = lax.rem(py + k, ny) // Y_LO
        to_y.append(send(out_y.at[goal], in_y.at[py], y_send.at[k], y_recv.at[k], at_y(k)))

    for copy in cross.values():
        copy.wait_recv()

    def project(k, total):
        cut = pl.ds(pl.multiple_of(k * 512, 512), 512)
        return total + jnp.dot(tok[:, cut], gathered[cut, :], preferred_element_type=F32)

    projected = lax.fori_loop(0, tok.shape[1] // 512, project, jnp.zeros((ROWS, KV), F32)) * inv_rms
    for h in range(KH):
        head = projected[:, h * HD : (h + 1) * HD]
        turned = head * cosine + pltpu.roll(head, HD // 2, 1) * sine
        keys_ref[:, h * HD : (h + 1) * HD] = turned.astype(BF16)

    for copy in to_z:
        copy.wait_recv()
    total = in_z[0].astype(F32)
    for k in range(1, nz):
        total = total + in_z[k].astype(F32)
    final_y[y_lo] = total
    pieces = []
    for k in range(1, Y_LO):
        target = device(px, y_hi * Y_LO + lax.rem(y_lo + k, Y_LO), pz, core)
        pieces.append(send(final_y.at[y_lo], final_y.at[y_lo], fy_send.at[k], fy_recv.at[k], target))
    for copy in to_y:
        copy.wait_recv()
    total = in_y[0].astype(F32)
    for k in range(1, ny):
        total = total + in_y[k].astype(F32)
    final_z[pz] = total
    for k in range(1, nz):
        pieces.append(send(final_z.at[pz], final_z.at[pz], fz_send.at[k], fz_recv.at[k], at_z(k)))
    for copy in pieces:
        copy.wait_recv()

    gain = gain_ref[...]
    dots = jnp.zeros((ROWS, 128), F32)
    for half, final in enumerate((final_y, final_z)):
        for s in range(2):
            value = final[:, s].reshape(ROWS, 128) * scale
            cols = slice(half * 256 + s * 128, half * 256 + (s + 1) * 128)
            weight_grad_ref[:, cols] = value * gain
            dots = dots + value * weight_ref[:, cols].astype(F32)
    column = jnp.sum(dots, axis=1, keepdims=True)
    gain_grad_ref[...] = jnp.broadcast_to(column, (ROWS, ROWS)).T[0:1, :]

    for copy in started:
        copy.wait_send()

    @pl.when(y_lo == 0)
    def _():
        for copy in far_copies(-1):
            copy.wait_send()

    @pl.when(y_lo == Y_LO - 1)
    def _():
        for copy in far_copies(1):
            copy.wait_send()


def local(tokens, norm_gain, key_weight, key_grad):
    rows, width = tokens.shape
    narrow_size = lax.axis_size("narrow")
    wide_size = lax.axis_size("wide")
    nx = narrow_size // 4
    ny = 2 * Y_LO
    nz = wide_size // Y_LO
    ry, rz = ROWS // Y_LO, ROWS // nz
    scale = 1.0 / math.sqrt(rows * narrow_size * wide_size)
    gain = norm_gain.astype(F32)[:, None]
    gained = (gain * key_weight.astype(F32)).astype(BF16)
    first_row = (lax.axis_index("wide") * narrow_size + lax.axis_index("narrow")) * rows
    position = ((first_row + jnp.arange(rows, dtype=jnp.int32)) % SEQ).astype(F32)
    halves = (jnp.arange(HD, dtype=jnp.int32) % (HD // 2)).astype(F32)
    frequency = rope_base ** (-2.0 * halves / HD)
    angle = position[:, None] * frequency[None, :]
    cosine = jnp.cos(angle)
    sine = jnp.sin(angle) * jnp.where(jnp.arange(HD) < HD // 2, -1.0, 1.0)[None, :]

    vmem = pl.BlockSpec(memory_space=pltpu.VMEM)
    dma = pltpu.SemaphoreType.DMA
    steps_x, steps_y, steps_z = nx // 2, ny // 2, nz // 2
    keys, weight_grad, gain_grad = pl.pallas_call(
        functools.partial(kernel, nx, nz, scale),
        out_shape=(
            jax.ShapeDtypeStruct((rows, KV), BF16),
            jax.ShapeDtypeStruct((ROWS, KV), F32),
            jax.ShapeDtypeStruct((1, ROWS), F32),
        ),
        in_specs=[pl.BlockSpec(memory_space=pl.ANY)] + [vmem] * 6,
        out_specs=(vmem, vmem, vmem),
        scratch_shapes=[
            pltpu.VMEM((rows, width), BF16),
            pltpu.VMEM((2 * nx, 2 * ROWS, 128), BF16),
            pltpu.VMEM((2 * ROWS, KV), BF16),
            pltpu.VMEM((width, KV), BF16),
            pltpu.VMEM((2, ny, nx, ry, 128), BF16),
            pltpu.VMEM((2, nz, 2 * nx, rz, 128), BF16),
            pltpu.VMEM((2, 2, steps_y, nx, ry, 128), BF16),
            pltpu.VMEM((2, 2, steps_z, 2 * nx, rz, 128), BF16),
            pltpu.VMEM((nx, 2, ry + 2 * rz, 128), BF16),
            pltpu.VMEM((nx, 2, ry + 2 * rz, 128), BF16),
            pltpu.VMEM((nz, 2, ry, 128), BF16),
            pltpu.VMEM((2, 2, rz, 128), BF16),
            pltpu.VMEM((ny, 2, rz, 128), BF16),
            pltpu.VMEM((Y_LO, 2, ry, 128), F32),
            pltpu.VMEM((nz, 2, rz, 128), F32),
            dma(()),
            dma((2 * nx,)),
            dma((2 * nx + 1,)), dma((2 * nx + 1,)),
            dma((2, nx)), dma((2, nx)),
            dma((max(Y_LO // 2, 1),)), dma(()),
            dma((2, 2, steps_x)), dma((2, 2, steps_x)),
            dma((2, 2, 2, max(steps_y, steps_z))), dma((2, 2, 2, max(steps_y, steps_z))),
            dma((nx,)), dma((nx,)),
            dma((nz,)), dma((nz,)),
            dma((ny,)), dma((ny,)),
            dma((Y_LO,)), dma((Y_LO,)),
            dma((nz,)), dma((nz,)),
        ],
        compiler_params=pltpu.CompilerParams(
            collective_id=0, has_side_effects=True, vmem_limit_bytes=48 * 1024 * 1024
        ),
    )(tokens, gained, key_grad, cosine, sine, key_weight, gain)
    return (keys, weight_grad, gain_grad.reshape(ROWS))


def solution(mesh):
    return jax.shard_map(
        local,
        mesh=mesh,
        in_specs=(
            P(("wide", "narrow"), None),
            P("narrow"),
            P("narrow", None),
            P(("wide", "narrow"), None),
        ),
        out_specs=(P(("wide", "narrow"), None), P("narrow", None), P("narrow")),
        check_vma=False,
    )
```

time: 579 us -> 79.3 us (0.14)
  the two profiles are of different devices: /device:TPU:1 before, /device:TPU:32 now
where the time goes in v2:
time: 79.3 us; the launch traced here: 79.1 us
  Pallas kernels  73.2 us (92%)
  local copies, waits for them, and re-layouts  4.02 us (5%)
  other arithmetic  1.11 us (1%)
    pallas_call x1, Pallas kernels, local(): pl.pallas_call(functools.partial(kernel, nx, nz, scale), out_shape=(jax.S...  73.2 us
    unnamed x9, local copies, waits for them, and re-layouts  3.91 us

profile of v2, /device:TPU:32, one launch (start us, length us, event | category | flops | bytes accessed | tf_op | source)
XLA Modules:
  0.0 79.1 jit_solution(15440660613189753726)
XLA Ops:
  0.6 0.0 copy-start.1
  0.7 0.7 convert_bitcast_fusion
  1.4 0.1 copy.7.gain_ref
  1.5 0.3 fusion
  1.8 0.0 copy-done.1
  1.8 0.0 copy-start.2
  1.8 0.1 multiply_convert_fusion.gained_ref
  1.9 0.8 %copy-done.2 = bf16[128,512]{1,0:T(8,128)(2,1)S(1)} copy-done((bf16[128,512]{1,0:T(8,128)(2,1)S(1)}, bf16[128,512]{1,0:T(8,128)(2,1)}, u32[]{:S(2)}) %copy-start.2) | copy-done | bytes 131096
  2.7 0.0 copy-start
  2.7 1.2 %copy-done = bf16[128,4096]{1,0:T(8,128)(2,1)S(1)} copy-done((bf16[128,4096]{1,0:T(8,128)(2,1)S(1)}, bf16[128,4096]{1,0:T(8,128)(2,1)}, u32[]{:S(2)}) %copy-start) | copy-done | bytes 1048600
  3.9 73.2 %shard_map.67 = (bf16[128,512]{1,0:T(8,128)(2,1)S(1)}, f32[128,512]{1,0:T(8,128)S(1)}, f32[1,128]{1,0:T(1,128)S(1)}) custom-call(bf16[128,4096]{1,0:T(8,128)(2,1)S(1)} %copy-done, bf16[128,512]{1,0:T(8,128)(2,1)S(1)} %multiply_convert_fusion.gained_ref, bf16[128,512]{1,0:T(8,128)(2,1)S(1)} %copy-done.2, f32[128,128]{1,0:T(8,128)S(1)} %get-tuple-element.10.cos_ref, ...), custom_call_target="tpu_custom_call" | custom-call | tf_op jit(solution)/shard_map/pallas_call | solution.py:350
  77.2 0.7 copy.11
  77.8 0.7 copy.12
  78.6 0.5 copy.13
  (2 shorter events, 0.0 us)
Async XLA Ops:
  0.6 1.2 %copy-start.1 = (bf16[128,512]{1,0:T(8,128)(2,1)S(1)}, bf16[128,512]{1,0:T(8,128)(2,1)}, u32[]{:S(2)}) copy-start(bf16[128,512]{1,0:T(8,128)(2,1)} %weight_ref.1) | copy-start | bytes 393220
  1.8 0.9 %copy-start.2 = (bf16[128,512]{1,0:T(8,128)(2,1)S(1)}, bf16[128,512]{1,0:T(8,128)(2,1)}, u32[]{:S(2)}) copy-start(bf16[128,512]{1,0:T(8,128)(2,1)} %key_grad_ref.1) | copy-start | bytes 393220
  2.7 1.2 %copy-start = (bf16[128,4096]{1,0:T(8,128)(2,1)S(1)}, bf16[128,4096]{1,0:T(8,128)(2,1)}, u32[]{:S(2)}) copy-start(bf16[128,4096]{1,0:T(8,128)(2,1)} %tokens_hbm.1) | copy-start | bytes 3145732

commit v3 on v2

v3 whole, which is shorter than its diff:
```python
import functools
import math

import jax
import jax.numpy as jnp
from jax import lax
from jax.experimental import pallas as pl
from jax.experimental.pallas import tpu as pltpu
from jax.sharding import PartitionSpec as P

KH = 4
HD = 128
KV = 512
SEQ = 4096
Y_LO = 4
ROWS = 128
PARTS = 2
RING_PLAN = {
    "mid": ((0, 1),), "start": (), 1: ((0, 2),), 2: ((0, 3), (1, 1)), 3: ((0, 4), (1, 2)),
    "end": ((1, 3),), "near": ((1, 4),), "far": (),
}

rope_base = 500000.0
norm_eps = 1e-05
MESH = pl.DeviceIdType.MESH
F32 = jnp.float32
BF16 = jnp.bfloat16


def chain_lengths(size):
    return (size // 2, size - 1 - size // 2)


def offset_groups(size):
    far_first = sorted(range(size), key=lambda o: (-min(o, size - o), o))
    count = size // PARTS
    return [far_first[g * count : (g + 1) * count] for g in range(PARTS)]


def kernel(
    nx, nz, scale,
    tokens_hbm, weight_hbm, key_grad_hbm, cos_ref, sin_ref, gain_ref,
    keys_ref, weight_grad_ref, gain_grad_ref,
    tok, mixed, weight, key_grad, turned_weight, proj, other, grads, gathered, part_y, part_z, chain_y, chain_z,
    out_x, in_x, in_z, out_y, in_y, final_y, final_z,
    local_sem, own_sem, pair_send, pair_recv, proj_send, proj_recv, far_send, far_recv,
    ring_send, ring_recv, chain_send, chain_recv,
    x_send, x_recv, z_send, z_recv, y_send, y_recv, fy_send, fy_recv, fz_send, fz_recv,
):
    ny = 2 * Y_LO
    wide = lax.axis_index("wide")
    narrow = lax.axis_index("narrow")
    core = lax.rem(narrow, 2)
    px = lax.rem(narrow // 2, nx)
    y_hi = narrow // (2 * nx)
    y_lo = lax.rem(wide, Y_LO)
    pz = wide // Y_LO
    py = y_hi * Y_LO + y_lo
    half_cols = KV // 2
    ky = half_cols // Y_LO
    kz = half_cols // nz
    groups = offset_groups(nx)
    group = nx // PARTS
    half_rows = ROWS // 2

    def device(x, y, z, c):
        return (z * Y_LO + lax.rem(y, Y_LO), ((y // Y_LO) * nx + x) * 2 + c)

    def at_x(k):
        return device(lax.rem(px + k + nx, nx), py, pz, core)

    def at_y(k):
        return device(px, lax.rem(py + k + ny, ny), pz, core)

    def at_z(k):
        return device(px, py, lax.rem(pz + k + nz, nz), core)

    sibling = device(px, py, pz, 1 - core)
    started = []

    def remote(src, dst, send_sem, recv_sem, target):
        return pltpu.make_async_remote_copy(
            src_ref=src, dst_ref=dst, send_sem=send_sem, recv_sem=recv_sem,
            device_id=target, device_id_type=MESH,
        )

    def send(src, dst, send_sem, recv_sem, target):
        copy = remote(src, dst, send_sem, recv_sem, target)
        copy.start()
        started.append(copy)
        return copy

    def shard(stream, offset, half):
        s = next(g for g in range(PARTS) if offset in groups[g])
        start = (stream * group + groups[s].index(offset)) * ROWS + half * half_rows
        return gathered.at[s, start : start + half_rows, :]

    barrier = pltpu.get_barrier_semaphore()
    partners = [sibling] + [at_x(k) for k in (1, -1)] + [at_z(k) for k in (1, -1)]
    partners += [at_y(k * sign) for k in range(1, max(Y_LO // 2, 1) + 1) for sign in (1, -1)]
    for partner in partners:
        pl.semaphore_signal(barrier, inc=1, device_id=partner, device_id_type=MESH)

    loads = []
    for i, (src, dst) in enumerate(((tokens_hbm, tok), (key_grad_hbm, key_grad), (weight_hbm, weight))):
        copy = pltpu.make_async_copy(src, dst, local_sem.at[i])
        copy.start()
        loads.append(copy)
    own_rows = pl.ds(pl.multiple_of(core * ROWS, ROWS), ROWS)

    highs = (y_hi, 1 - y_hi)

    def block_cols(stream, offset, c):
        hi = highs[stream]
        x = lax.rem(px + offset, nx)
        return pl.ds(pl.multiple_of(((hi * nx + x) * 2 + c) * ROWS, ROWS), ROWS)

    own_loads = {}
    for s in range(PARTS):
        for stream in range(2):
            for i, offset in enumerate(groups[s]):
                b = stream * group + i
                copy = pltpu.make_async_copy(
                    tokens_hbm.at[:, block_cols(stream, offset, core)],
                    mixed.at[s, own_rows, b * 128 : (b + 1) * 128],
                    own_sem.at[s, b],
                )
                copy.start()
                own_loads[s, b] = copy

    pl.semaphore_wait(barrier, len(partners))

    pair = {}
    for s in range(PARTS):
        for stream in range(2):
            for i, offset in enumerate(groups[s]):
                b = stream * group + i
                pair[s, b] = send(
                    tokens_hbm.at[:, block_cols(stream, offset, 1 - core)],
                    mixed.at[s, own_rows, b * 128 : (b + 1) * 128],
                    pair_send.at[s, b], pair_recv.at[s, b], sibling,
                )

    loads[2].wait()
    gain_cols = jnp.broadcast_to(gain_ref[...], (ROWS, ROWS)).T
    for h in range(KH):
        part = (weight[:, h * HD : (h + 1) * HD].astype(F32) * gain_cols).astype(BF16)
        for half in range(2):
            shard(0, 0, half)[:, h * HD : (h + 1) * HD] = part[half * half_rows : (half + 1) * half_rows]

    def far_copies(sign):
        return [
            remote(
                shard(0, 0, half), shard(1, 0, half),
                far_send.at[i, half], far_recv.at[half], at_y(sign * (i + 1)),
            )
            for half in range(2)
            for i in range(Y_LO // 2)
        ]

    @pl.when(y_lo == 0)
    def _():
        for copy in far_copies(-1):
            copy.start()

    @pl.when(y_lo == Y_LO - 1)
    def _():
        for copy in far_copies(1):
            copy.start()

    long_x, short_x = chain_lengths(nx)
    ring_steps = [[long_x, short_x], [short_x, long_x]]
    ring = {}

    def ring_step(stream, way, t, half):
        steps = ring_steps[stream][way]
        if t > steps or steps == 0:
            return
        sign = 1 - 2 * way
        if t > 0:
            ring[stream, way, t - 1, half].wait_recv()
        if t < steps:
            index = (stream, way, t, half)
            ring[index] = send(
                shard(stream, (-sign * t) % nx, half), shard(stream, (-sign * (t + 1)) % nx, half),
                ring_send.at[index], ring_recv.at[index], at_x(sign),
            )

    def ring_round(stream, t):
        for half in range(2):
            for way in range(2):
                ring_step(stream, way, t, half)

    visited = set()

    def ring_point(name):
        for item in RING_PLAN[name]:
            if item not in visited:
                ring_round(*item)
                visited.add(item)

    def ring_far_start():
        for half in range(2):
            remote(
                shard(0, 0, half), shard(1, 0, half), far_send.at[0, 0], far_recv.at[half], sibling
            ).wait_recv()
            for way in range(2):
                ring_step(1, way, 0, half)

    ring_round(0, 0)

    cosine, sine = cos_ref[...], sin_ref[...]
    loads[0].wait()
    squares = jnp.zeros((ROWS, 128), F32)
    for j in range(4 * nx):
        piece = tok[:, j * 128 : (j + 1) * 128].astype(F32)
        squares = squares + piece * piece
    mean = jnp.sum(squares, axis=1, keepdims=True) * (1.0 / tok.shape[1])
    inv_rms = lax.rsqrt(mean + norm_eps)
    loads[1].wait()
    for h in range(KH):
        part = key_grad[:, h * HD : (h + 1) * HD].astype(F32)
        turned = (part * cosine - pltpu.roll(part, HD // 2, 1) * sine) * inv_rms
        grads[core, h * HD : (h + 1) * HD, :] = turned.T.astype(BF16)
    pair["grads"] = send(grads.at[core], grads.at[core], pair_send.at[PARTS, 0], pair_recv.at[PARTS, 0], sibling)

    axes = ((ny, py, at_y, part_y, chain_y), (nz, pz, at_z, part_z, chain_z))
    chains = {}

    def chain_steps(size, way, s):
        return chain_lengths(size)[(way + s) % 2]

    def chain_step(axis, way, s, t):
        size, place, at, part, chain = axes[axis]
        steps = chain_steps(size, way, s)
        if t >= steps:
            return
        sign = 1 - 2 * way
        goal = lax.rem(place + sign * (steps - t) + size, size)
        if t > 0:
            chains[axis, way, s, t - 1].wait_recv()
            part[s, goal] = part[s, goal] + chain[way, s, t - 1]
        index = (axis, way, s, t)
        chains[index] = send(
            part.at[s, goal], chain.at[way, s, t], chain_send.at[index], chain_recv.at[index], at(sign)
        )

    def chain_round(s, t):
        for axis in range(2):
            for way in range(2):
                chain_step(axis, way, s, t)

    pair["grads"].wait_recv()
    both = jnp.concatenate([grads[0], grads[1]], axis=1)
    for s in range(PARTS):
        for b in range(2 * group):
            own_loads[s, b].wait()
            pair[s, b].wait_recv()
        for p in range(group):
            value = jnp.dot(both, mixed[s, :, p * 256 : (p + 1) * 256], preferred_element_type=F32).astype(BF16)
            for side in range(2):
                b = 2 * p + side
                stream, i = divmod(b, group)
                block = value[:, side * 128 : (side + 1) * 128]
                for k in range(Y_LO):
                    part_y[s, highs[stream] * Y_LO + k, i] = block[k * ky : (k + 1) * ky]
                for k in range(nz):
                    part_z[s, k, b] = block[half_cols + k * kz : half_cols + (k + 1) * kz]
        chain_round(s, 0)
        if s == 0:
            ring_point("mid")
    ring_far_start()
    ring_point("start")

    to_x = {}

    def chain_end(s):
        for axis in range(2):
            size, place, _, part, chain = axes[axis]
            total = part[s, place].astype(F32)
            for way in range(2):
                steps = chain_steps(size, way, s)
                if steps > 0:
                    chains[axis, way, s, steps - 1].wait_recv()
                    total = total + chain[way, s, steps - 1].astype(F32)
            total = total.astype(BF16)
            for i, offset in enumerate(groups[s]):
                if axis == 0:
                    out_x[offset, :ky, :] = total[i]
                else:
                    for hi in range(2):
                        out_x[offset, ky + hi * kz : ky + (hi + 1) * kz, :] = total[hi * group + i]
        for offset in groups[s]:
            if offset:
                to_x[offset] = send(
                    out_x.at[offset], in_x.at[offset], x_send.at[offset], x_recv.at[offset], at_x(offset)
                )

    longest = max(ny, nz) // 2
    for t in range(1, longest):
        for s in range(PARTS):
            chain_round(s, t)
        ring_point(t)
    for t in range(1, nx):
        if (0, t) not in visited:
            ring_round(0, t)
            visited.add((0, t))
    for s in range(PARTS):
        chain_end(s)
    ring_point("end")

    def project(s):
        value = jnp.dot(mixed[s], gathered[s], preferred_element_type=F32).reshape(2, ROWS, KV)
        if s == PARTS - 1:
            proj[...] = value
        else:
            proj[...] += value

    for s in range(PARTS - 1, 0, -1):
        project(s)
    ring_point("near")

    total = out_x[0].astype(F32)
    for k in range(1, nx):
        to_x[k].wait_recv()
        total = total + in_x[k].astype(F32)
    total = total.astype(BF16)
    in_z[pz] = total[:ky]
    for hi in range(2):
        out_y[hi] = total[ky + hi * kz : ky + (hi + 1) * kz]
    in_y[py] = out_y[0]

    to_z = []
    for k in range(1, nz):
        to_z.append(send(in_z.at[pz], in_z.at[pz], z_send.at[k], z_recv.at[k], at_z(k)))
    to_y = []
    for k in range(1, ny):
        goal = lax.rem(lax.rem(py + k, ny) // Y_LO + y_hi, 2)
        to_y.append(send(out_y.at[goal], in_y.at[py], y_send.at[k], y_recv.at[k], at_y(k)))

    ring_point("far")
    for stream in range(2):
        for t in range(1, nx):
            if (stream, t) not in visited:
                ring_round(stream, t)
    project(0)
    halves = send(proj.at[1 - core], other, proj_send, proj_recv, sibling)
    for h in range(KH):
        turned_weight[h * HD : (h + 1) * HD, :] = weight[:, h * HD : (h + 1) * HD].astype(F32).T

    for copy in to_z:
        copy.wait_recv()
    total = in_z[0].astype(F32)
    for k in range(1, nz):
        total = total + in_z[k].astype(F32)
    final_y[y_lo] = total.astype(BF16)
    pieces = []
    for k in range(1, Y_LO):
        target = device(px, y_hi * Y_LO + lax.rem(y_lo + k, Y_LO), pz, core)
        pieces.append(send(final_y.at[y_lo], final_y.at[y_lo], fy_send.at[k], fy_recv.at[k], target))
    for copy in to_y:
        copy.wait_recv()
    total = in_y[0].astype(F32)
    for k in range(1, ny):
        total = total + in_y[k].astype(F32)
    final_z[pz] = total.astype(BF16)
    for k in range(1, nz):
        pieces.append(send(final_z.at[pz], final_z.at[pz], fz_send.at[k], fz_recv.at[k], at_z(k)))

    halves.wait_recv()
    for h in range(KH):
        cols = slice(h * HD, (h + 1) * HD)
        part = (proj[core, :, cols] + other[:, cols]) * inv_rms
        turned = part * cosine + pltpu.roll(part, HD // 2, 1) * sine
        keys_ref[:, cols] = turned.astype(BF16)

    for copy in pieces:
        copy.wait_recv()

    gain = gain_ref[...]
    dots = jnp.zeros((ROWS, 128), F32)
    for h in range(KH):
        if h < 2:
            value = final_y[h * Y_LO // 2 : (h + 1) * Y_LO // 2].reshape(HD, 128).astype(F32) * scale
        else:
            value = final_z[(h - 2) * nz // 2 : (h - 1) * nz // 2].reshape(HD, 128).astype(F32) * scale
        dots = dots + value * turned_weight[h * HD : (h + 1) * HD, :]
        weight_grad_ref[:, h * HD : (h + 1) * HD] = (value * gain).T
    gain_grad_ref[...] = jnp.sum(dots, axis=0, keepdims=True)

    for copy in started:
        copy.wait_send()

    @pl.when(y_lo == 0)
    def _():
        for copy in far_copies(-1):
            copy.wait_send()

    @pl.when(y_lo == Y_LO - 1)
    def _():
        for copy in far_copies(1):
            copy.wait_send()


def local(tokens, norm_gain, key_weight, key_grad):
    rows, width = tokens.shape
    narrow_size = lax.axis_size("narrow")
    wide_size = lax.axis_size("wide")
    nx = narrow_size // 4
    ny = 2 * Y_LO
    nz = wide_size // Y_LO
    ky, kz = KV // 2 // Y_LO, KV // 2 // nz
    group = nx // PARTS
    scale = 1.0 / math.sqrt(rows * narrow_size * wide_size)
    gain = norm_gain.astype(F32).reshape(1, ROWS)
    first_row = (lax.axis_index("wide") * narrow_size + lax.axis_index("narrow")) * rows
    position = ((first_row + jnp.arange(rows, dtype=jnp.int32)) % SEQ).astype(F32)
    halves = (jnp.arange(HD, dtype=jnp.int32) % (HD // 2)).astype(F32)
    frequency = rope_base ** (-2.0 * halves / HD)
    angle = position[:, None] * frequency[None, :]
    cosine = jnp.cos(angle)
    sine = jnp.sin(angle) * jnp.where(jnp.arange(HD) < HD // 2, -1.0, 1.0)[None, :]

    vmem = pl.BlockSpec(memory_space=pltpu.VMEM)
    hbm = pl.BlockSpec(memory_space=pltpu.HBM)
    dma = pltpu.SemaphoreType.DMA
    steps_x, steps_y, steps_z = nx // 2, ny // 2, nz // 2
    keys, weight_grad, gain_grad = pl.pallas_call(
        functools.partial(kernel, nx, nz, scale),
        out_shape=(
            jax.ShapeDtypeStruct((rows, KV), BF16),
            jax.ShapeDtypeStruct((ROWS, KV), F32),
            jax.ShapeDtypeStruct((1, ROWS), F32),
        ),
        in_specs=[hbm] * 3 + [vmem] * 3,
        out_specs=(vmem, vmem, vmem),
        scratch_shapes=[
            pltpu.VMEM((rows, width), BF16),
            pltpu.VMEM((PARTS, 2 * ROWS, 2 * group * 128), BF16),
            pltpu.VMEM((ROWS, KV), BF16),
            pltpu.VMEM((rows, KV), BF16),
            pltpu.VMEM((KV, ROWS), F32),
            pltpu.VMEM((2, ROWS, KV), F32),
            pltpu.VMEM((ROWS, KV), F32),
            pltpu.VMEM((2, KV, ROWS), BF16),
            pltpu.VMEM((PARTS, 2 * group * ROWS, KV), BF16),
            pltpu.VMEM((PARTS, ny, group, ky, 128), BF16),
            pltpu.VMEM((PARTS, nz, 2 * group, kz, 128), BF16),
            pltpu.VMEM((2, PARTS, steps_y, group, ky, 128), BF16),
            pltpu.VMEM((2, PARTS, steps_z, 2 * group, kz, 128), BF16),
            pltpu.VMEM((nx, ky + 2 * kz, 128), BF16),
            pltpu.VMEM((nx, ky + 2 * kz, 128), BF16),
            pltpu.VMEM((nz, ky, 128), BF16),
            pltpu.VMEM((2, kz, 128), BF16),
            pltpu.VMEM((ny, kz, 128), BF16),
            pltpu.VMEM((Y_LO, ky, 128), BF16),
            pltpu.VMEM((nz, kz, 128), BF16),
            dma((3,)),
            dma((PARTS, 2 * group)),
            dma((PARTS + 1, 2 * group)), dma((PARTS + 1, 2 * group)),
            dma(()), dma(()),
            dma((max(Y_LO // 2, 1), 2)), dma((2,)),
            dma((2, 2, steps_x, 2)), dma((2, 2, steps_x, 2)),
            dma((2, 2, PARTS, max(steps_y, steps_z))), dma((2, 2, PARTS, max(steps_y, steps_z))),
            dma((nx,)), dma((nx,)),
            dma((nz,)), dma((nz,)),
            dma((ny,)), dma((ny,)),
            dma((Y_LO,)), dma((Y_LO,)),
            dma((nz,)), dma((nz,)),
        ],
        compiler_params=pltpu.CompilerParams(
            collective_id=0, has_side_effects=True, vmem_limit_bytes=55_300_000
        ),
    )(tokens, key_weight, key_grad, cosine, sine, gain)
    return (keys, weight_grad, gain_grad.reshape(ROWS))


def solution(mesh):
    return jax.shard_map(
        local,
        mesh=mesh,
        in_specs=(
            P(("wide", "narrow"), None),
            P("narrow"),
            P("narrow", None),
            P(("wide", "narrow"), None),
        ),
        out_specs=(P(("wide", "narrow"), None), P("narrow", None), P("narrow")),
        check_vma=False,
    )
```

time: 79.3 us -> 72.4 us (0.913)
  the two profiles are of different devices: /device:TPU:32 before, /device:TPU:4 now
where the time goes in v3:
time: 72.4 us; the launch traced here: 72.2 us
  Pallas kernels  67.7 us (94%)
  local copies, waits for them, and re-layouts  2.77 us (4%)
  other arithmetic  1.03 us (1%)
    pallas_call x1, Pallas kernels, local(): pl.pallas_call(functools.partial(kernel, nx, nz, scale), out_shape=(jax.S...  67.7 us
    unnamed x7, local copies, waits for them, and re-layouts  2.77 us

profile of v3, /device:TPU:4, one launch (start us, length us, event | category | flops | bytes accessed | tf_op | source)
XLA Modules:
  0.0 72.2 jit_solution(9980958333647514320)
XLA Ops:
  0.6 0.0 copy-start
  0.7 0.7 bitcast_convert_fusion.gain_ref
  1.4 0.3 fusion
  1.7 0.0 copy-done
  1.7 0.0 copy-start.1
  1.7 0.9 %copy-done.1 = bf16[128,512]{1,0:T(8,128)(2,1)S(1)} copy-done((bf16[128,512]{1,0:T(8,128)(2,1)S(1)}, bf16[128,512]{1,0:T(8,128)(2,1)}, u32[]{:S(2)}) %copy-start.1) | copy-done | bytes 131096
  2.6 67.7 %shard_map.67 = (bf16[128,512]{1,0:T(8,128)(2,1)S(1)}, f32[128,512]{1,0:T(8,128)S(1)}, f32[1,128]{1,0:T(1,128)S(1)}) custom-call(bf16[128,4096]{1,0:T(8,128)(2,1)} %tokens_hbm.1, bf16[128,512]{1,0:T(8,128)(2,1)S(1)} %copy-done, bf16[128,512]{1,0:T(8,128)(2,1)S(1)} %copy-done.1, f32[128,128]{1,0:T(8,128)S(1)} %get-tuple-element.10.cos_ref, ...), custom_call_target="tpu_custom_call" | custom-call | tf_op jit(solution)/shard_map/pallas_call | solution.py:428
  70.3 0.7 copy.10
  71.0 0.7 copy.11
  71.7 0.5 copy.12
  (2 shorter events, 0.0 us)
Async XLA Ops:
  0.6 1.1 %copy-start = (bf16[128,512]{1,0:T(8,128)(2,1)S(1)}, bf16[128,512]{1,0:T(8,128)(2,1)}, u32[]{:S(2)}) copy-start(bf16[128,512]{1,0:T(8,128)(2,1)} %weight_hbm.1) | copy-start | bytes 393220
  1.7 0.9 %copy-start.1 = (bf16[128,512]{1,0:T(8,128)(2,1)S(1)}, bf16[128,512]{1,0:T(8,128)(2,1)}, u32[]{:S(2)}) copy-start(bf16[128,512]{1,0:T(8,128)(2,1)} %key_grad_hbm.1) | copy-start | bytes 393220

commit v4 on v3

--- a/solution.py
+++ b/solution.py
@@ -15,10 +15,12 @@
 Y_LO = 4
 ROWS = 128
 PARTS = 2
+PROJECT_AT = ("summed_x", "summed_x")
 RING_PLAN = {
-    "mid": ((0, 1),), "start": (), 1: ((0, 2),), 2: ((0, 3), (1, 1)), 3: ((0, 4), (1, 2)),
-    "end": ((1, 3),), "near": ((1, 4),), "far": (),
+    "mid": (), "start": ((0, 1),), 1: ((0, 2),), 2: ((1, 1),), 3: ((0, 3), (1, 2)),
+    "end": ((0, 4), (1, 3)), "near": (), "far": ((1, 4),),
 }
+LIFT_AT = (3, "end", "near", "far")
 
 rope_base = 500000.0
 norm_eps = 1e-05
@@ -44,7 +46,7 @@
     tok, mixed, weight, key_grad, turned_weight, proj, other, grads, gathered, part_y, part_z, chain_y, chain_z,
     out_x, in_x, in_z, out_y, in_y, final_y, final_z,
     local_sem, own_sem, pair_send, pair_recv, proj_send, proj_recv, far_send, far_recv,
-    ring_send, ring_recv, chain_send, chain_recv,
+    ring_send, ring_recv, lift_send, lift_recv, hop_sem, chain_send, chain_recv,
     x_send, x_recv, z_send, z_recv, y_send, y_recv, fy_send, fy_recv, fz_send, fz_recv,
 ):
     ny = 2 * Y_LO
@@ -90,10 +92,17 @@
         started.append(copy)
         return copy
 
+    parity = lax.rem(pz, 2)
+    pieces_of = (2, 1)
+
     def shard(stream, offset, half):
         s = next(g for g in range(PARTS) if offset in groups[g])
-        start = (stream * group + groups[s].index(offset)) * ROWS + half * half_rows
-        return gathered.at[s, start : start + half_rows, :]
+        start = (stream * group + groups[s].index(offset)) * ROWS
+        if stream == 1:
+            rows = pl.ds(pl.multiple_of(start + parity * half_rows, half_rows), half_rows)
+        else:
+            rows = slice(start + half * half_rows, start + (half + 1) * half_rows)
+        return gathered.at[s, rows, :]
 
     barrier = pltpu.get_barrier_semaphore()
     partners = [sibling] + [at_x(k) for k in (1, -1)] + [at_z(k) for k in (1, -1)]
@@ -130,6 +139,24 @@
 
     pl.semaphore_wait(barrier, len(partners))
 
+    rounds = nx // 2 - 1
+    passed = [0]
+
+    def pass_on(upto):
+        while passed[0] < upto:
+            r = passed[0]
+            pl.semaphore_wait(hop_sem.at[r], 2)
+            passed[0] = r + 1
+            if r + 1 < rounds:
+                greet(r + 1)
+
+    def greet(r):
+        for k in (1, -1):
+            pl.semaphore_signal(hop_sem.at[r], inc=1, device_id=at_x(k), device_id_type=MESH)
+
+    if rounds > 0:
+        greet(0)
+
     pair = {}
     for s in range(PARTS):
         for stream in range(2):
@@ -140,74 +167,6 @@
                     mixed.at[s, own_rows, b * 128 : (b + 1) * 128],
                     pair_send.at[s, b], pair_recv.at[s, b], sibling,
                 )
-
-    loads[2].wait()
-    gain_cols = jnp.broadcast_to(gain_ref[...], (ROWS, ROWS)).T
-    for h in range(KH):
-        part = (weight[:, h * HD : (h + 1) * HD].astype(F32) * gain_cols).astype(BF16)
-        for half in range(2):
-            shard(0, 0, half)[:, h * HD : (h + 1) * HD] = part[half * half_rows : (half + 1) * half_rows]
-
-    def far_copies(sign):
-        return [
-            remote(
-                shard(0, 0, half), shard(1, 0, half),
-                far_send.at[i, half], far_recv.at[half], at_y(sign * (i + 1)),
-            )
-            for half in range(2)
-            for i in range(Y_LO // 2)
-        ]
-
-    @pl.when(y_lo == 0)
-    def _():
-        for copy in far_copies(-1):
-            copy.start()
-
-    @pl.when(y_lo == Y_LO - 1)
-    def _():
-        for copy in far_copies(1):
-            copy.start()
-
-    long_x, short_x = chain_lengths(nx)
-    ring_steps = [[long_x, short_x], [short_x, long_x]]
-    ring = {}
-
-    def ring_step(stream, way, t, half):
-        steps = ring_steps[stream][way]
-        if t > steps or steps == 0:
-            return
-        sign = 1 - 2 * way
-        if t > 0:
-            ring[stream, way, t - 1, half].wait_recv()
-        if t < steps:
-            index = (stream, way, t, half)
-            ring[index] = send(
-                shard(stream, (-sign * t) % nx, half), shard(stream, (-sign * (t + 1)) % nx, half),
-                ring_send.at[index], ring_recv.at[index], at_x(sign),
-            )
-
-    def ring_round(stream, t):
-        for half in range(2):
-            for way in range(2):
-                ring_step(stream, way, t, half)
-
-    visited = set()
-
-    def ring_point(name):
-        for item in RING_PLAN[name]:
-            if item not in visited:
-                ring_round(*item)
-                visited.add(item)
-
-    def ring_far_start():
-        for half in range(2):
-            remote(
-                shard(0, 0, half), shard(1, 0, half), far_send.at[0, 0], far_recv.at[half], sibling
-            ).wait_recv()
-            for way in range(2):
-                ring_step(1, way, 0, half)
-
-    ring_round(0, 0)
 
     cosine, sine = cos_ref[...], sin_ref[...]
     loads[0].wait()
@@ -223,6 +182,86 @@
         turned = (part * cosine - pltpu.roll(part, HD // 2, 1) * sine) * inv_rms
         grads[core, h * HD : (h + 1) * HD, :] = turned.T.astype(BF16)
     pair["grads"] = send(grads.at[core], grads.at[core], pair_send.at[PARTS, 0], pair_recv.at[PARTS, 0], sibling)
+
+    loads[2].wait()
+    gain_cols = jnp.broadcast_to(gain_ref[...], (ROWS, ROWS)).T
+    for h in range(KH):
+        part = (weight[:, h * HD : (h + 1) * HD].astype(F32) * gain_cols).astype(BF16)
+        for half in range(2):
+            shard(0, 0, half)[:, h * HD : (h + 1) * HD] = part[half * half_rows : (half + 1) * half_rows]
+
+    own_half = gathered.at[
+        PARTS - 1,
+        pl.ds(pl.multiple_of(groups[PARTS - 1].index(0) * ROWS + parity * half_rows, half_rows), half_rows),
+        :,
+    ]
+
+    def far_copies(sign):
+        return [
+            remote(own_half, shard(1, 0, 0), far_send.at[i], far_recv, at_y(sign * (i + 1)))
+            for i in range(Y_LO // 2)
+        ]
+
+    @pl.when(y_lo == 0)
+    def _():
+        for copy in far_copies(-1):
+            copy.start()
+
+    @pl.when(y_lo == Y_LO - 1)
+    def _():
+        for copy in far_copies(1):
+            copy.start()
+
+    long_x, short_x = chain_lengths(nx)
+    ring_steps = [[long_x, short_x], [short_x, long_x]]
+    ring = {}
+
+    def ring_step(stream, way, t, half):
+        steps = ring_steps[stream][way]
+        if t > steps or steps == 0:
+            return
+        sign = 1 - 2 * way
+        if t > 0:
+            ring[stream, way, t - 1, half].wait_recv()
+        if t < steps:
+            index = (stream, way, t, half)
+            ring[index] = send(
+                shard(stream, (-sign * t) % nx, half), shard(stream, (-sign * (t + 1)) % nx, half),
+                ring_send.at[index], ring_recv.at[index], at_x(sign),
+            )
+
+    lifts = {}
+    waiting = []
+
+    def lift(offset):
+        rows = shard(1, offset, 0)
+        toward = 1 - 2 * (next(g.index(offset) for g in groups if offset in g) % 2)
+        lifts[offset] = send(rows, rows, lift_send.at[offset], lift_recv.at[offset], at_z(toward))
+
+    def ring_round(stream, t):
+        for half in range(pieces_of[stream]):
+            for way in range(2):
+                ring_step(stream, way, t, half)
+                if stream == 1 and 0 < t <= ring_steps[1][way]:
+                    waiting.append((-(1 - 2 * way) * t) % nx)
+
+    visited = set()
+
+    def ring_point(name):
+        for item in RING_PLAN[name]:
+            if item not in visited:
+                ring_round(*item)
+                visited.add(item)
+        while waiting and name in LIFT_AT:
+            lift(waiting.pop(0))
+
+    def ring_far_start():
+        remote(own_half, shard(1, 0, 0), far_send.at[0], far_recv, sibling).wait_recv()
+        for way in range(2):
+            ring_step(1, way, 0, 0)
+        waiting.append(0)
+
+    ring_round(0, 0)
 
     axes = ((ny, py, at_y, part_y, chain_y), (nz, pz, at_z, part_z, chain_z))
     chains = {}
@@ -267,6 +306,7 @@
                 for k in range(nz):
                     part_z[s, k, b] = block[half_cols + k * kz : half_cols + (k + 1) * kz]
         chain_round(s, 0)
+        pass_on(min(s + 1, rounds))
         if s == 0:
             ring_point("mid")
     ring_far_start()
@@ -301,24 +341,45 @@
         for s in range(PARTS):
             chain_round(s, t)
         ring_point(t)
-    for t in range(1, nx):
-        if (0, t) not in visited:
-            ring_round(0, t)
-            visited.add((0, t))
+    pass_on(rounds)
     for s in range(PARTS):
         chain_end(s)
     ring_point("end")
 
     def project(s):
+        for offset in groups[s]:
+            lifts[offset].wait_recv()
         value = jnp.dot(mixed[s], gathered[s], preferred_element_type=F32).reshape(2, ROWS, KV)
         if s == PARTS - 1:
             proj[...] = value
         else:
             proj[...] += value
 
-    for s in range(PARTS - 1, 0, -1):
-        project(s)
     ring_point("near")
+
+    def ring_rest():
+        for stream in range(2):
+            for t in range(1, nx):
+                if (stream, t) not in visited:
+                    visited.add((stream, t))
+                    ring_round(stream, t)
+        while waiting:
+            lift(waiting.pop(0))
+
+    def project_at(point):
+        for s in range(PARTS - 1, -1, -1):
+            if PROJECT_AT[s] == point:
+                if s == 0 or point == "summed_all":
+                    ring_point("far")
+                    ring_rest()
+                project(s)
+                if s == 0:
+                    proj_copy.append(
+                        send(proj.at[1 - core], other, proj_send, proj_recv, sibling)
+                    )
+
+    proj_copy = []
+    project_at("chained")
 
     total = out_x[0].astype(F32)
     for k in range(1, nx):
@@ -338,13 +399,7 @@
         goal = lax.rem(lax.rem(py + k, ny) // Y_LO + y_hi, 2)
         to_y.append(send(out_y.at[goal], in_y.at[py], y_send.at[k], y_recv.at[k], at_y(k)))
 
-    ring_point("far")
-    for stream in range(2):
-        for t in range(1, nx):
-            if (stream, t) not in visited:
-                ring_round(stream, t)
-    project(0)
-    halves = send(proj.at[1 - core], other, proj_send, proj_recv, sibling)
+    project_at("summed_x")
     for h in range(KH):
         turned_weight[h * HD : (h + 1) * HD, :] = weight[:, h * HD : (h + 1) * HD].astype(F32).T
 
@@ -367,7 +422,8 @@
     for k in range(1, nz):
         pieces.append(send(final_z.at[pz], final_z.at[pz], fz_send.at[k], fz_recv.at[k], at_z(k)))
 
-    halves.wait_recv()
+    project_at("summed_all")
+    proj_copy[0].wait_recv()
     for h in range(KH):
         cols = slice(h * HD, (h + 1) * HD)
         part = (proj[core, :, cols] + other[:, cols]) * inv_rms
@@ -459,8 +515,10 @@
             dma((PARTS, 2 * group)),
             dma((PARTS + 1, 2 * group)), dma((PARTS + 1, 2 * group)),
             dma(()), dma(()),
-            dma((max(Y_LO // 2, 1), 2)), dma((2,)),
+            dma((max(Y_LO // 2, 1),)), dma(()),
             dma((2, 2, steps_x, 2)), dma((2, 2, steps_x, 2)),
+            dma((nx,)), dma((nx,)),
+            pltpu.SemaphoreType.REGULAR((max(nx // 2 - 1, 1),)),
             dma((2, 2, PARTS, max(steps_y, steps_z))), dma((2, 2, PARTS, max(steps_y, steps_z))),
             dma((nx,)), dma((nx,)),
             dma((nz,)), dma((nz,)),

time: 72.4 us -> 65.8 us (0.909)
  the two profiles are of different devices: /device:TPU:4 before, /device:TPU:16 now
where the time goes in v4:
time: 65.8 us; the launch traced here: 65.6 us
  Pallas kernels  61.1 us (93%)
  local copies, waits for them, and re-layouts  2.77 us (4%)
  other arithmetic  1.03 us (2%)
  between operations  0.68 us (1%)
    pallas_call x1, Pallas kernels, local(): pl.pallas_call(functools.partial(kernel, nx, nz, scale), out_shape=(jax.S...  61.1 us
    unnamed x7, local copies, waits for them, and re-layouts  2.77 us

profile of v4, /device:TPU:16, one launch (start us, length us, event | category | flops | bytes accessed | tf_op | source)
XLA Modules:
  0.0 65.6 jit_solution(14078831687914124049)
XLA Ops:
  0.6 0.0 copy-start
  0.7 0.7 %bitcast_convert_fusion.gain_ref = f32[1,128]{1,0:T(1,128)S(1)} fusion(bf16[128]{0:T(256)(128)(2,1)} %param.5), kind=kLoop, calls=%fused_computation.13 | loop fusion | flops 128 | bytes 768 | tf_op jit(solution)/shard_map/reshape | solution.py:471
  1.4 0.3 fusion
  1.7 0.0 copy-done
  1.7 0.0 copy-start.1
  1.7 0.9 %copy-done.1 = bf16[128,512]{1,0:T(8,128)(2,1)S(1)} copy-done((bf16[128,512]{1,0:T(8,128)(2,1)S(1)}, bf16[128,512]{1,0:T(8,128)(2,1)}, u32[]{:S(2)}) %copy-start.1) | copy-done | bytes 131096
  2.6 61.1 %shard_map.67 = (bf16[128,512]{1,0:T(8,128)(2,1)S(1)}, f32[128,512]{1,0:T(8,128)S(1)}, f32[1,128]{1,0:T(1,128)S(1)}) custom-call(bf16[128,4096]{1,0:T(8,128)(2,1)} %tokens_hbm.1, bf16[128,512]{1,0:T(8,128)(2,1)S(1)} %copy-done, bf16[128,512]{1,0:T(8,128)(2,1)S(1)} %copy-done.1, f32[128,128]{1,0:T(8,128)S(1)} %get-tuple-element.10.cos_ref, ...), custom_call_target="tpu_custom_call" | custom-call | tf_op jit(solution)/shard_map/pallas_call | solution.py:484
  63.7 0.7 %copy.10 = bf16[128,512]{1,0:T(8,128)(2,1)} copy(bf16[128,512]{1,0:T(8,128)(2,1)S(1)} %get-tuple-element.16) | data formatting | bytes 262144
  64.4 0.7 %copy.11 = f32[128,512]{1,0:T(8,128)} copy(f32[128,512]{1,0:T(8,128)S(1)} %get-tuple-element.17) | data formatting | bytes 524288
  65.1 0.5 copy.12
  (2 shorter events, 0.0 us)
Async XLA Ops:
  0.6 1.1 %copy-start = (bf16[128,512]{1,0:T(8,128)(2,1)S(1)}, bf16[128,512]{1,0:T(8,128)(2,1)}, u32[]{:S(2)}) copy-start(bf16[128,512]{1,0:T(8,128)(2,1)} %weight_hbm.1) | copy-start | bytes 393220
  1.7 0.9 %copy-start.1 = (bf16[128,512]{1,0:T(8,128)(2,1)S(1)}, bf16[128,512]{1,0:T(8,128)(2,1)}, u32[]{:S(2)}) copy-start(bf16[128,512]{1,0:T(8,128)(2,1)} %key_grad_hbm.1) | copy-start | bytes 393220

commit v5 on v4

--- a/solution.py
+++ b/solution.py
@@ -17,7 +17,7 @@
 PARTS = 2
 PROJECT_AT = ("summed_x", "summed_x")
 RING_PLAN = {
-    "mid": (), "start": ((0, 1),), 1: ((0, 2),), 2: ((1, 1),), 3: ((0, 3), (1, 2)),
+    "mid": (), "start": ((0, 1),), 1: ((0, 2),), 2: ((1, 1), (0, 3)), 3: ((1, 2),),
     "end": ((0, 4), (1, 3)), "near": (), "far": ((1, 4),),
 }
 LIFT_AT = (3, "end", "near", "far")

time: 65.8 us -> 65.2 us (level)
  the two profiles are of different devices: /device:TPU:16 before, /device:TPU:32 now
where the time goes in v5:
time: 65.2 us; the launch traced here: 65 us
  Pallas kernels  60.5 us (93%)
  local copies, waits for them, and re-layouts  2.77 us (4%)
  other arithmetic  1.03 us (2%)
  between operations  0.68 us (1%)
    pallas_call x1, Pallas kernels, local(): pl.pallas_call(functools.partial(kernel, nx, nz, scale), out_shape=(jax.S...  60.5 us
    unnamed x7, local copies, waits for them, and re-layouts  2.77 us

profile of v5, /device:TPU:32, one launch (start us, length us, event | category | flops | bytes accessed | tf_op | source)
XLA Modules:
  0.0 65.0 jit_solution(11964841649857636831)
XLA Ops:
  0.6 0.0 copy-start
  0.7 0.7 %bitcast_convert_fusion.gain_ref = f32[1,128]{1,0:T(1,128)S(1)} fusion(bf16[128]{0:T(256)(128)(2,1)} %param.5), kind=kLoop, calls=%fused_computation.13 | loop fusion | flops 128 | bytes 768 | tf_op jit(solution)/shard_map/reshape | solution.py:471
  1.4 0.3 fusion
  1.7 0.0 copy-done
  1.7 0.0 copy-start.1
  1.7 0.9 %copy-done.1 = bf16[128,512]{1,0:T(8,128)(2,1)S(1)} copy-done((bf16[128,512]{1,0:T(8,128)(2,1)S(1)}, bf16[128,512]{1,0:T(8,128)(2,1)}, u32[]{:S(2)}) %copy-start.1) | copy-done | bytes 131096
  2.6 60.5 %shard_map.67 = (bf16[128,512]{1,0:T(8,128)(2,1)S(1)}, f32[128,512]{1,0:T(8,128)S(1)}, f32[1,128]{1,0:T(1,128)S(1)}) custom-call(bf16[128,4096]{1,0:T(8,128)(2,1)} %tokens_hbm.1, bf16[128,512]{1,0:T(8,128)(2,1)S(1)} %copy-done, bf16[128,512]{1,0:T(8,128)(2,1)S(1)} %copy-done.1, f32[128,128]{1,0:T(8,128)S(1)} %get-tuple-element.10.cos_ref, ...), custom_call_target="tpu_custom_call" | custom-call | tf_op jit(solution)/shard_map/pallas_call | solution.py:484
  63.1 0.7 %copy.10 = bf16[128,512]{1,0:T(8,128)(2,1)} copy(bf16[128,512]{1,0:T(8,128)(2,1)S(1)} %get-tuple-element.16) | data formatting | bytes 262144
  63.8 0.7 %copy.11 = f32[128,512]{1,0:T(8,128)} copy(f32[128,512]{1,0:T(8,128)S(1)} %get-tuple-element.17) | data formatting | bytes 524288
  64.5 0.5 copy.12
  (2 shorter events, 0.0 us)
Async XLA Ops:
  0.6 1.1 %copy-start = (bf16[128,512]{1,0:T(8,128)(2,1)S(1)}, bf16[128,512]{1,0:T(8,128)(2,1)}, u32[]{:S(2)}) copy-start(bf16[128,512]{1,0:T(8,128)(2,1)} %weight_hbm.1) | copy-start | bytes 393220
  1.7 0.9 %copy-start.1 = (bf16[128,512]{1,0:T(8,128)(2,1)S(1)}, bf16[128,512]{1,0:T(8,128)(2,1)}, u32[]{:S(2)}) copy-start(bf16[128,512]{1,0:T(8,128)(2,1)} %key_grad_hbm.1) | copy-start | bytes 393220
